TPU v7x, 32 devices: a whole 2x2x4 slice. The times are simulated.
32 devices in a mesh: seq: 8 (over y, x, core), tp: 4 (over z).
Axes of the slice: x: 2, y: 2, z: 4, core: 2. Of those that a mesh axis runs over, the one named last changes fastest.
Arguments:
- tokens: bfloat16 [128, 17, 1152], P('seq'), may hold values from -6 to 6
- cotangent: bfloat16 [128, 17, 1152], P('seq'), may hold values from -6 to 6
- caption: bfloat16 [4, 300, 1152], replicated, may hold values from -6 to 6
- condition: float32 [4, 1152], replicated, may hold values from -6 to 6
- frames: int32 [4], replicated, may hold values from 1 to 17, 44 in all
- cap_len: int32 [4], replicated, may hold values from 1 to 300, 600 in all
- clip_of: int32 [128], P('seq'), may hold values from 0 to 3
- w_qkv: bfloat16 [1152, 3, 1152], P('seq', None, 'tp'), may hold values from -0.1875 to 0.1875
- w_out: bfloat16 [1152, 1152], P('tp', 'seq'), may hold values from -0.375 to 0.375
- w_query2: bfloat16 [1152, 1152], P('seq', 'tp'), may hold values from -0.1875 to 0.1875
- w_kv2: bfloat16 [1152, 2, 1152], P('seq', None, 'tp'), may hold values from -0.1875 to 0.1875
- w_out2: bfloat16 [1152, 1152], P('tp', 'seq'), may hold values from -0.75 to 0.75
- w_up: bfloat16 [1152, 4608], P('seq', 'tp'), may hold values from -0.1875 to 0.1875
- w_down: bfloat16 [4608, 1152], P('tp', 'seq'), may hold values from -0.09375 to 0.09375
- w_ada: bfloat16 [1152, 6912], P('seq', 'tp'), may hold values from -0.1875 to 0.1875
Outputs:
- output: bfloat16 [128, 17, 1152], P('seq')
- d_tokens: bfloat16 [128, 17, 1152], P('seq')
- d_caption: float32 [4, 300, 1152], P(None, None, 'tp')
- d_condition: float32 [4, 1152], replicated
- d_w_qkv: float32 [1152, 3, 1152], P('seq', None, 'tp')
- d_w_out: float32 [1152, 1152], P('tp', 'seq')
- d_w_query2: float32 [1152, 1152], P('seq', 'tp')
- d_w_kv2: float32 [1152, 2, 1152], P('seq', None, 'tp')
- d_w_out2: float32 [1152, 1152], P('tp', 'seq')
- d_w_up: float32 [1152, 4608], P('seq', 'tp')
- d_w_down: float32 [4608, 1152], P('tp', 'seq')
- d_w_ada: float32 [1152, 6912], P('seq', 'tp')
Inputs may be any that keep to these rules, and one draw needn't show every extreme that they name: frames of each clip; they add up to 44 and one clip has 17. `cap_len`: live caption tokens of each clip, the first ones of its slots; they add up to 600 and one clip has 300.
All inputs are finite; a program needn't handle non-finite values.
Results may differ from a plain program's by a relative error of at most 0.024.
Values may be sent and summed in bfloat16 or wider, within the bound.
No kernel may reach another device: no remote copies, remote signals or barrier semaphores. Data moves between devices by JAX's collectives and lax.ppermute only.
A program may use at most 128 MiB of HBM per device.

v0:
```python
import jax
import jax.numpy as jnp
from jax import lax
from jax.sharding import PartitionSpec as P

HDIM = 72
CLIPS = 4
EPSILON = 1e-06
NEG_FILL = -1e30
HIGHEST = lax.Precision.HIGHEST


def normalize(rows):
    center = rows - jnp.mean(rows, -1, keepdims=True)
    return center * lax.rsqrt(jnp.mean(center * center, -1, keepdims=True) + EPSILON)


def modulate(rows, shift, scale):
    return normalize(rows) * (1.0 + scale[:, None, :]) + shift[:, None, :]


def total_rows(partial_value):
    return lax.psum(partial_value, "tp")


def frame_attention(triple, live, head_scale):
    raw = (
        jnp.einsum(
            "lfhe,lghe->lhfg", triple[:, :, 0], triple[:, :, 1], preferred_element_type=jnp.float32
        )
        * head_scale
    )
    probs = jax.nn.softmax(jnp.where(live[:, None, None, :], raw, NEG_FILL), axis=-1)
    result = jnp.einsum(
        "lhfg,lghe->lfhe",
        probs.astype(jnp.bfloat16),
        triple[:, :, 2],
        preferred_element_type=jnp.float32,
    )
    return (probs, result.astype(jnp.bfloat16))


def cross_scores(query, keys, clips, key_clip, key_live, head_scale):
    raw = jnp.einsum("rhe,khe->hrk", query, keys, preferred_element_type=jnp.float32) * head_scale
    allowed = (clips[:, None] == key_clip[None, :]) & key_live[None, :]
    return jnp.where(allowed[None], raw, NEG_FILL)


def shards(
    tokens,
    cotangent,
    caption,
    condition,
    frames,
    cap_len,
    clip_of,
    w_qkv,
    w_out,
    w_query2,
    w_kv2,
    w_out2,
    w_up,
    w_down,
    w_ada,
):
    seqs, fmax, width = tokens.shape
    row_count = seqs * fmax
    inner = w_qkv.shape[2]
    local_heads = inner // HDIM
    head_scale = HDIM ** (-0.5)
    full_qkv, full_out, full_query2, full_kv2, full_out2, full_up, full_down, full_ada = (
        lax.all_gather(w_qkv, "seq", axis=0, tiled=True),
        lax.all_gather(w_out, "seq", axis=1, tiled=True),
        lax.all_gather(w_query2, "seq", axis=0, tiled=True),
        lax.all_gather(w_kv2, "seq", axis=0, tiled=True),
        lax.all_gather(w_out2, "seq", axis=1, tiled=True),
        lax.all_gather(w_up, "seq", axis=0, tiled=True),
        lax.all_gather(w_down, "seq", axis=1, tiled=True),
        lax.all_gather(w_ada, "seq", axis=0, tiled=True),
    )
    qkv_matrix = full_qkv.reshape(width, 3 * inner)
    kv_matrix = full_kv2.reshape(width, 2 * inner)
    scaled = jax.nn.silu(condition).astype(jnp.bfloat16)
    mod_part = jnp.dot(scaled, full_ada, preferred_element_type=jnp.float32)
    mods = lax.all_gather(mod_part, "tp", axis=1, tiled=True).reshape(CLIPS, 6, width)
    clip_ids = jnp.arange(CLIPS)
    clip_hot = clip_of[:, None] == clip_ids[None, :]
    seq_mods = jnp.sum(jnp.where(clip_hot[:, :, None, None], mods[None], 0.0), 1)
    seq_frames = jnp.sum(jnp.where(clip_hot, frames[None, :], 0), 1)
    live = jnp.arange(fmax)[None, :] < seq_frames[:, None]
    own_live = live.astype(jnp.float32)[:, :, None]
    own_hot = clip_hot.astype(jnp.float32)
    key_count = caption.shape[0] * caption.shape[1]
    key_clip = jnp.arange(key_count) // caption.shape[1]
    key_len = jnp.sum(jnp.where(key_clip[:, None] == clip_ids[None, :], cap_len[None, :], 0), 1)
    key_live = jnp.arange(key_count) % caption.shape[1] < key_len
    row_clip = jnp.repeat(clip_of, fmax)
    block_seqs = min(32, seqs)
    blocks = seqs // block_seqs
    block_rows = block_seqs * fmax
    block_clip = row_clip.reshape(blocks, block_rows)
    own_input = tokens.astype(jnp.float32)
    attn_in = (
        modulate(own_input, seq_mods[:, 0], seq_mods[:, 1])
        .astype(jnp.bfloat16)
        .reshape(row_count, width)
    )
    triple = (
        jnp.dot(attn_in, qkv_matrix, preferred_element_type=jnp.float32)
        .astype(jnp.bfloat16)
        .reshape(seqs, fmax, 3, local_heads, HDIM)
    )
    probs, frame_out = frame_attention(triple, live, head_scale)
    frame_out = frame_out.reshape(row_count, inner)
    branch_one = total_rows(
        jnp.dot(frame_out, full_out, preferred_element_type=jnp.float32).reshape(seqs, fmax, width)
    )
    first = own_input + seq_mods[:, 2][:, None, :] * branch_one
    first_low = first.astype(jnp.bfloat16).reshape(row_count, width)
    cross_query = (
        jnp.dot(first_low, full_query2, preferred_element_type=jnp.float32)
        .astype(jnp.bfloat16)
        .reshape(blocks, block_rows, local_heads, HDIM)
    )
    cross_kv = (
        jnp.dot(caption.reshape(key_count, width), kv_matrix, preferred_element_type=jnp.float32)
        .astype(jnp.bfloat16)
        .reshape(key_count, 2, local_heads, HDIM)
    )
    cross_key = cross_kv[:, 0]
    cross_value = cross_kv[:, 1]

    def cross_block(pair):
        query, clips = pair
        scores = cross_scores(query, cross_key, clips, key_clip, key_live, head_scale)
        top = jnp.max(scores, -1, keepdims=True)
        weights = jnp.exp(scores - top)
        denom = jnp.sum(weights, -1, keepdims=True)
        block_out = jnp.einsum(
            "hrk,khe->rhe",
            (weights / denom).astype(jnp.bfloat16),
            cross_value,
            preferred_element_type=jnp.float32,
        )
        return (block_out.astype(jnp.bfloat16), (top + jnp.log(denom))[..., 0])

    cross_out, cross_lse = lax.map(cross_block, (cross_query, block_clip))
    cross_out = cross_out.reshape(row_count, inner)
    second = first + total_rows(
        jnp.dot(cross_out, full_out2, preferred_element_type=jnp.float32).reshape(seqs, fmax, width)
    )
    mlp_in = (
        modulate(second, seq_mods[:, 3], seq_mods[:, 4])
        .astype(jnp.bfloat16)
        .reshape(row_count, width)
    )
    hidden_pre = jnp.dot(mlp_in, full_up, preferred_element_type=jnp.float32)
    hidden = jax.nn.gelu(hidden_pre, approximate=True).astype(jnp.bfloat16)
    branch_three = total_rows(
        jnp.dot(hidden, full_down, preferred_element_type=jnp.float32).reshape(seqs, fmax, width)
    )
    third = second + seq_mods[:, 5][:, None, :] * branch_three
    output = (third * own_live).astype(jnp.bfloat16)
    grad_three = cotangent.astype(jnp.float32) * own_live
    d_branch3 = (
        (seq_mods[:, 5][:, None, :] * grad_three).astype(jnp.bfloat16).reshape(row_count, width)
    )
    grad_down = jnp.einsum("rk,rd->kd", hidden, d_branch3, preferred_element_type=jnp.float32)
    d_hidden = jnp.einsum("rd,kd->rk", d_branch3, full_down, preferred_element_type=jnp.float32)
    gelu_pull = jax.vjp(lambda value: jax.nn.gelu(value, approximate=True), hidden_pre)[1]
    d_pre = gelu_pull(d_hidden)[0].astype(jnp.bfloat16)
    grad_up = jnp.einsum("rd,rk->dk", mlp_in, d_pre, preferred_element_type=jnp.float32)
    d_mlp = total_rows(
        jnp.einsum("rk,dk->rd", d_pre, full_up, preferred_element_type=jnp.float32).reshape(
            seqs, fmax, width
        )
    )
    second_pull = jax.vjp(modulate, second, seq_mods[:, 3], seq_mods[:, 4])[1]
    norm_two, d_shift2, d_scale2 = second_pull(d_mlp)
    grad_two = grad_three + norm_two
    d_branch2 = grad_two.astype(jnp.bfloat16).reshape(row_count, width)
    grad_out2 = jnp.einsum("rc,rd->cd", cross_out, d_branch2, preferred_element_type=jnp.float32)
    d_cross = (
        jnp.einsum("rd,cd->rc", d_branch2, full_out2, preferred_element_type=jnp.float32)
        .astype(jnp.bfloat16)
        .reshape(blocks, block_rows, local_heads, HDIM)
    )

    def cross_back(carry, item):
        key_sum, value_sum = carry
        query, clips, block_lse, grad_block = item
        scores = cross_scores(query, cross_key, clips, key_clip, key_live, head_scale)
        weights = jnp.exp(scores - block_lse[..., None])
        value_sum = value_sum + jnp.einsum(
            "hrk,rhe->khe",
            weights.astype(jnp.bfloat16),
            grad_block,
            preferred_element_type=jnp.float32,
        )
        grad_weights = jnp.einsum(
            "rhe,khe->hrk", grad_block, cross_value, preferred_element_type=jnp.float32
        )
        grad_scores = (
            weights * (grad_weights - jnp.sum(weights * grad_weights, -1, keepdims=True))
        ).astype(jnp.bfloat16)
        grad_query = (
            jnp.einsum("hrk,khe->rhe", grad_scores, cross_key, preferred_element_type=jnp.float32)
            * head_scale
        ).astype(jnp.bfloat16)
        key_sum = (
            key_sum
            + jnp.einsum("hrk,rhe->khe", grad_scores, query, preferred_element_type=jnp.float32)
            * head_scale
        )
        return ((key_sum, value_sum), grad_query)

    zero_keys = jnp.zeros((key_count, local_heads, HDIM), jnp.float32)
    (key_grad, value_grad), d_query = lax.scan(
        cross_back, (zero_keys, zero_keys), (cross_query, block_clip, cross_lse, d_cross)
    )
    d_query = d_query.reshape(row_count, inner)
    grad_query2 = jnp.einsum("rd,rc->dc", first_low, d_query, preferred_element_type=jnp.float32)
    grad_one = grad_two + total_rows(
        jnp.einsum("rc,dc->rd", d_query, full_query2, preferred_element_type=jnp.float32).reshape(
            seqs, fmax, width
        )
    )
    d_branch1 = (
        (seq_mods[:, 2][:, None, :] * grad_one).astype(jnp.bfloat16).reshape(row_count, width)
    )
    grad_out = jnp.einsum("rc,rd->cd", frame_out, d_branch1, preferred_element_type=jnp.float32)
    d_frame = (
        jnp.einsum("rd,cd->rc", d_branch1, full_out, preferred_element_type=jnp.float32)
        .astype(jnp.bfloat16)
        .reshape(seqs, fmax, local_heads, HDIM)
    )
    d_value = jnp.einsum(
        "lhfg,lfhe->lghe", probs.astype(jnp.bfloat16), d_frame, preferred_element_type=jnp.float32
    )
    d_probs = jnp.einsum(
        "lfhe,lghe->lhfg", d_frame, triple[:, :, 2], preferred_element_type=jnp.float32
    )
    d_scores = (probs * (d_probs - jnp.sum(probs * d_probs, -1, keepdims=True))).astype(
        jnp.bfloat16
    )
    d_queries = (
        jnp.einsum("lhfg,lghe->lfhe", d_scores, triple[:, :, 1], preferred_element_type=jnp.float32)
        * head_scale
    )
    d_keys = (
        jnp.einsum("lhfg,lfhe->lghe", d_scores, triple[:, :, 0], preferred_element_type=jnp.float32)
        * head_scale
    )
    d_triple = (
        jnp.stack([d_queries, d_keys, d_value], 2)
        .astype(jnp.bfloat16)
        .reshape(row_count, 3 * inner)
    )
    grad_qkv = jnp.einsum(
        "rd,rc->dc", attn_in, d_triple, preferred_element_type=jnp.float32
    ).reshape(width, 3, inner)
    d_attn = total_rows(
        jnp.einsum("rc,dc->rd", d_triple, qkv_matrix, preferred_element_type=jnp.float32).reshape(
            seqs, fmax, width
        )
    )
    first_pull = jax.vjp(modulate, own_input, seq_mods[:, 0], seq_mods[:, 1])[1]
    norm_one, d_shift1, d_scale1 = first_pull(d_attn)
    d_tokens = (grad_one + norm_one).astype(jnp.bfloat16)
    d_gate1 = jnp.sum(grad_one * branch_one, 1)
    d_gate2 = jnp.sum(grad_three * branch_three, 1)
    seq_terms = jnp.stack([d_shift1, d_scale1, d_gate1, d_shift2, d_scale2, d_gate2], 1)
    d_mods = jnp.einsum("lc,ljd->cjd", own_hot, seq_terms, precision=HIGHEST).reshape(
        CLIPS, 6 * width
    )
    kv_grad = jnp.stack([key_grad, value_grad], 1)
    kv_total, mods_total = (
        lax.psum(kv_grad.astype(jnp.bfloat16), "seq").astype(jnp.float32),
        lax.psum(d_mods.astype(jnp.bfloat16), "seq").astype(jnp.float32),
    )
    col_count = mods_total.shape[1] // lax.axis_size("tp")
    mod_cols = lax.dynamic_slice_in_dim(mods_total, lax.axis_index("tp") * col_count, col_count, 1)
    seq_rows = w_ada.shape[0]
    seq_start = lax.axis_index("seq") * seq_rows
    scaled_rows = lax.dynamic_slice_in_dim(scaled, seq_start, seq_rows, 1).astype(jnp.float32)
    grad_ada = jnp.einsum("cd,ck->dk", scaled_rows, mod_cols, precision=HIGHEST)
    silu_pull = jax.vjp(jax.nn.silu, condition)[1]
    cond_part = silu_pull(
        jnp.einsum("ck,dk->cd", mod_cols, full_ada.astype(jnp.float32), precision=HIGHEST)
    )[0]
    d_condition = lax.psum(cond_part, "tp")
    kv_low = kv_total.astype(jnp.bfloat16).reshape(key_count, 2 * inner)
    caption_rows = lax.dynamic_slice_in_dim(
        caption.reshape(key_count, width), seq_start, seq_rows, 1
    )
    grad_kv2 = jnp.einsum(
        "kd,kc->dc", caption_rows, kv_low, preferred_element_type=jnp.float32
    ).reshape(seq_rows, 2, inner)
    caption_part = jnp.einsum(
        "kc,dc->kd", kv_low, kv_matrix, preferred_element_type=jnp.float32
    ).reshape(caption.shape)
    d_caption = lax.psum_scatter(
        caption_part.astype(jnp.bfloat16), "tp", scatter_dimension=2, tiled=True
    ).astype(jnp.float32)
    summed = (
        lax.psum_scatter(
            grad_qkv.astype(jnp.bfloat16), "seq", scatter_dimension=0, tiled=True
        ).astype(jnp.float32),
        lax.psum_scatter(
            grad_out.astype(jnp.bfloat16), "seq", scatter_dimension=1, tiled=True
        ).astype(jnp.float32),
        lax.psum_scatter(
            grad_query2.astype(jnp.bfloat16), "seq", scatter_dimension=0, tiled=True
        ).astype(jnp.float32),
        lax.psum_scatter(
            grad_out2.astype(jnp.bfloat16), "seq", scatter_dimension=1, tiled=True
        ).astype(jnp.float32),
        lax.psum_scatter(
            grad_up.astype(jnp.bfloat16), "seq", scatter_dimension=0, tiled=True
        ).astype(jnp.float32),
        lax.psum_scatter(
            grad_down.astype(jnp.bfloat16), "seq", scatter_dimension=1, tiled=True
        ).astype(jnp.float32),
    )
    return (
        output,
        d_tokens,
        d_caption,
        d_condition,
        summed[0],
        summed[1],
        summed[2],
        grad_kv2,
        summed[3],
        summed[4],
        summed[5],
        grad_ada,
    )


def solution(mesh):
    return jax.shard_map(
        shards,
        mesh=mesh,
        in_specs=(
            P("seq", None, None),
            P("seq", None, None),
            P(),
            P(),
            P(),
            P(),
            P("seq"),
            P("seq", None, "tp"),
            P("tp", "seq"),
            P("seq", "tp"),
            P("seq", None, "tp"),
            P("tp", "seq"),
            P("seq", "tp"),
            P("tp", "seq"),
            P("seq", "tp"),
        ),
        out_specs=(
            P("seq", None, None),
            P("seq", None, None),
            P(None, None, "tp"),
            P(),
            P("seq", None, "tp"),
            P("tp", "seq"),
            P("seq", "tp"),
            P("seq", None, "tp"),
            P("tp", "seq"),
            P("seq", "tp"),
            P("tp", "seq"),
            P("seq", "tp"),
        ),
        check_vma=False,
    )
```

profile of v0, /device:TPU:0, one launch (start us, length us, event | category | flops | bytes accessed | tf_op | source)
XLA Modules:
  0.0 1068.3 jit_solution(13612882484881826433)
XLA Ops:
  14.8 15.0 %all_gather.30 = bf16[288,1152]{0,1:T(8,128)(2,1)S(1)} all-gather(bf16[288,144]{0,1:T(8,128)(2,1)S(1)} %copy-done.45), channel_id=1, replica_groups=mesh['seq'=8,'tp'=4] {'seq'}, dimensions={1}, use_global_device_ids=true | all-gather | bytes 746496 | tf_op jit(solution)/shard_map/all_gather | solution.py:73
  29.7 13.7 %all_gather.32 = bf16[1152,288]{1,0:T(8,128)(2,1)S(1)} all-gather(bf16[144,288]{1,0:T(8,128)(2,1)S(1)} %copy-done.46), channel_id=1, replica_groups=mesh['seq'=8,'tp'=4] {'seq'}, dimensions={0}, use_global_device_ids=true | all-gather | bytes 746496 | tf_op jit(solution)/shard_map/all_gather | solution.py:74
  43.4 11.3 %all_gather.33 = bf16[288,1152]{0,1:T(8,128)(2,1)} all-gather(bf16[288,144]{0,1:T(8,128)(2,1)S(1)} %copy-done.47), channel_id=1, replica_groups=mesh['seq'=8,'tp'=4] {'seq'}, dimensions={1}, use_global_device_ids=true | all-gather | bytes 746496 | tf_op jit(solution)/shard_map/all_gather | solution.py:76
  64.2 21.8 %all-gather.7.cloned.1.call-done = bf16[1152,1728]{1,0:T(8,128)(2,1)} async-done(((bf16[144,1728]{1,0:T(8,128)(2,1)}), bf16[1152,1728]{1,0:T(8,128)(2,1)}) %all-gather.7.cloned.1.call-update) | async-done | bytes 3981328 | tf_op jit(solution)/shard_map/all_gather | solution.py:79
  88.8 13.4 %all-gather = f32[4,1728,4]{1,2,0:T(4,128)S(1)} all-gather(f32[1,1728,4]{1,2,0:T(4,128)S(1)} %convolution_bitcast_fusion), channel_id=1, replica_groups=mesh['seq'=8,'tp'=4] {'tp'}, dimensions={0}, use_global_device_ids=true | all-gather | bytes 138240 | tf_op jit(solution)/shard_map/all_gather | solution.py:85
  123.3 5.6 copy.152
  128.9 5.6 convolution_convert_fusion.4
  134.5 63.4 %all-reduce.8.cloned.1.call-done = f32[16,17,1152]{2,1,0:T(8,128)} async-done(((f32[16,17,1152]{2,1,0:T(8,128)}), f32[16,17,1152]{2,1,0:T(8,128)}) %all-reduce.8.cloned.1.call-update) | async-done | bytes 1253392 | tf_op jit(solution)/shard_map/psum | solution.py:23
  212.2 73.3 %all-reduce.10.cloned.1.call-done = f32[16,17,1152]{2,1,0:T(8,128)} async-done(((f32[16,17,1152]{2,1,0:T(8,128)}), f32[16,17,1152]{2,1,0:T(8,128)}) %all-reduce.10.cloned.1.call-update) | async-done | bytes 1253392 | tf_op jit(solution)/shard_map/psum | solution.py:23
  295.4 21.2 %all-gather.15.cloned.1.call-done = bf16[1152,1152]{0,1:T(8,128)(2,1)} async-done(((bf16[1152,144]{0,1:T(8,128)(2,1)}), bf16[1152,1152]{0,1:T(8,128)(2,1)}) %all-gather.15.cloned.1.call-update) | async-done | bytes 2654224 | tf_op jit(solution)/shard_map/all_gather | solution.py:78
  320.7 28.1 %all-gather.13.cloned.1.call-done = bf16[1152,1152]{1,0:T(8,128)(2,1)} async-done(((bf16[144,1152]{1,0:T(8,128)(2,1)}), bf16[1152,1152]{1,0:T(8,128)(2,1)}) %all-gather.13.cloned.1.call-update) | async-done | bytes 2654224 | tf_op jit(solution)/shard_map/all_gather | solution.py:77
  348.8 5.0 fusion.36
  359.8 75.4 %all-reduce.12.cloned.1.call-done = f32[16,17,1152]{2,1,0:T(8,128)} async-done(((f32[16,17,1152]{2,1,0:T(8,128)}), f32[16,17,1152]{2,1,0:T(8,128)}) %all-reduce.12.cloned.1.call-update) | async-done | bytes 1253392 | tf_op jit(solution)/shard_map/psum | solution.py:23
  476.0 59.8 %all-reduce.14.cloned.1.call-done = f32[16,17,1152]{2,1,0:T(8,128)} async-done(((f32[16,17,1152]{2,1,0:T(8,128)}), f32[16,17,1152]{2,1,0:T(8,128)}) %all-reduce.14.cloned.1.call-update) | async-done | bytes 1253392 | tf_op jit(solution)/shard_map/psum | solution.py:23
  604.5 6.6 convolution_convert_fusion.2
  611.1 23.5 %reduce-scatter.16.cloned.1.call-done = bf16[288,144]{0,1:T(8,128)(2,1)} async-done(((bf16[288,1152]{0,1:T(8,128)(2,1)}), bf16[288,144]{0,1:T(8,128)(2,1)}) %reduce-scatter.16.cloned.1.call-update) | async-done | bytes 82960 | tf_op jit(solution)/shard_map/reduce_scatter | solution.py:315
  636.2 36.7 %reduce-scatter.14.cloned.1.call-done = bf16[144,288]{1,0:T(8,128)(2,1)} async-done(((bf16[1152,288]{1,0:T(8,128)(2,1)}), bf16[144,288]{1,0:T(8,128)(2,1)}) %reduce-scatter.14.cloned.1.call-update) | async-done | bytes 82960 | tf_op jit(solution)/shard_map/reduce_scatter | solution.py:312
  674.4 37.7 %reduce-scatter.12.cloned.1.call-done = bf16[288,144]{0,1:T(8,128)(2,1)} async-done(((bf16[288,1152]{0,1:T(8,128)(2,1)}), bf16[288,144]{0,1:T(8,128)(2,1)}) %reduce-scatter.12.cloned.1.call-update) | async-done | bytes 82960 | tf_op jit(solution)/shard_map/reduce_scatter | solution.py:309
  713.7 45.6 %reduce-scatter.18.cloned.1.call-done = bf16[144,1152]{1,0:T(8,128)(2,1)} async-done(((bf16[1152,1152]{1,0:T(8,128)(2,1)}), bf16[144,1152]{1,0:T(8,128)(2,1)}) %reduce-scatter.18.cloned.1.call-update) | async-done | bytes 331792 | tf_op jit(solution)/shard_map/reduce_scatter | solution.py:318
  761.2 45.7 %reduce-scatter.20.cloned.1.call-done = bf16[1152,144]{0,1:T(8,128)(2,1)} async-done(((bf16[1152,1152]{0,1:T(8,128)(2,1)}), bf16[1152,144]{0,1:T(8,128)(2,1)}) %reduce-scatter.20.cloned.1.call-update) | async-done | bytes 331792 | tf_op jit(solution)/shard_map/reduce_scatter | solution.py:321
  808.7 135.2 %all-reduce.18.cloned.1.call-done = (f32[16,17,1152]{2,1,0:T(8,128)}, f32[16,17,1152]{2,1,0:T(8,128)}) async-done(((f32[16,17,1152]{2,1,0:T(8,128)}, f32[16,17,1152]{2,1,0:T(8,128)}), (f32[16,17,1152]{2,1,0:T(8,128)}, f32[16,17,1152]{2,1,0:T(8,128)})) %all-reduce.18.cloned.1.call-update) | async-done | bytes 2506768 | tf_op jit(solution)/shard_map/psum | solution.py:23
  951.2 24.9 %psum.70 = bf16[4,6912]{1,0:T(4,128)(2,1)S(1)} all-reduce(bf16[4,6912]{1,0:T(4,128)(2,1)S(1)} %bitcast.198), channel_id=1, replica_groups=mesh['seq'=8,'tp'=4] {'seq'}, use_global_device_ids=true, to_apply=%region_31.32 | all-reduce | flops 27648 | bytes 110592 | tf_op jit(solution)/shard_map/psum | solution.py:279
  979.5 17.6 %psum.71 = f32[4,1152]{1,0:T(4,128)} all-reduce(f32[4,1152]{1,0:T(4,128)S(1)} %fusion.68), channel_id=1, replica_groups=mesh['seq'=8,'tp'=4] {'tp'}, use_global_device_ids=true, to_apply=%region_32.33 | all-reduce | flops 4608 | bytes 36864 | tf_op jit(solution)/shard_map/psum | solution.py:291
  1001.1 57.7 %reduce-scatter.8.cloned.1.call-done = bf16[4,300,288]{1,2,0:T(8,128)(2,1)} async-done(((bf16[4,300,1152]{1,2,0:T(8,128)(2,1)}), bf16[4,300,288]{1,2,0:T(8,128)(2,1)}) %reduce-scatter.8.cloned.1.call-update) | async-done | bytes 691216 | tf_op jit(solution)/shard_map/reduce_scatter | solution.py:302
  (301 shorter events, 209.3 us)
Async XLA Ops:
  7.2 52.7 %all-gather.9.cloned.1.call-start = ((), (), s32[]{:S(2)}) async-start(), calls=%async_computation.8 | async-start | bytes 2985984 | tf_op jit(solution)/shard_map/all_gather | solution.py:72
  8.0 78.0 %all-gather.7.cloned.1.call-start = ((), (), s32[]{:S(2)}) async-start(), calls=%async_computation.7 | async-start | bytes 4644864 | tf_op jit(solution)/shard_map/all_gather | solution.py:79
  8.7 114.6 %all-gather.11.cloned.1.call-start = ((), (), s32[]{:S(2)}) async-start(), calls=%async_computation.10 | async-start | bytes 1990656 | tf_op jit(solution)/shard_map/all_gather | solution.py:75
  9.5 188.4 %all-reduce.8.cloned.1.call-start = ((), (), s32[]{:S(2)}) async-start(), calls=%async_computation.9 | async-start | bytes 3538944 | tf_op jit(solution)/shard_map/psum | solution.py:23
  29.7 90.2 %copy-start.9 = (bf16[288,1152]{0,1:T(8,128)(2,1)}, bf16[288,1152]{0,1:T(8,128)(2,1)S(1)}, u32[]{:S(2)}) copy-start(bf16[288,1152]{0,1:T(8,128)(2,1)S(1)} %all_gather.30) | copy-start | bytes 1990660
  43.4 156.5 %copy-start.10 = (bf16[1152,288]{1,0:T(8,128)(2,1)}, bf16[1152,288]{1,0:T(8,128)(2,1)S(1)}, u32[]{:S(2)}) copy-start(bf16[1152,288]{1,0:T(8,128)(2,1)S(1)} %all_gather.32) | copy-start | bytes 1990660
  103.3 182.3 %copy-start.31 = (f32[16,1152]{1,0:T(8,128)}, f32[16,1152]{1,0:T(8,128)S(1)}, u32[]{:S(2)}) copy-start(f32[16,1152]{1,0:T(8,128)S(1)} %get-tuple-element.159) | copy-start | bytes 221188
  103.3 185.1 %copy-start.36 = (f32[16,1152]{1,0:T(8,128)}, f32[16,1152]{1,0:T(8,128)S(1)}, u32[]{:S(2)}) copy-start(f32[16,1152]{1,0:T(8,128)S(1)} %get-tuple-element.154) | copy-start | bytes 221188
  121.9 163.6 %all-reduce.10.cloned.1.call-start = ((), (), s32[]{:S(2)}) async-start(), calls=%async_computation.11 | async-start | bytes 3538944 | tf_op jit(solution)/shard_map/psum | solution.py:23
  210.8 105.8 %all-gather.15.cloned.1.call-start = ((), (), s32[]{:S(2)}) async-start(), calls=%async_computation.13 | async-start | bytes 2985984 | tf_op jit(solution)/shard_map/all_gather | solution.py:78
  211.4 137.4 %all-gather.13.cloned.1.call-start = ((), (), s32[]{:S(2)}) async-start(), calls=%async_computation.12 | async-start | bytes 2985984 | tf_op jit(solution)/shard_map/all_gather | solution.py:77
  212.2 223.0 %all-reduce.12.cloned.1.call-start = ((), (), s32[]{:S(2)}) async-start(), calls=%async_computation.14 | async-start | bytes 3538944 | tf_op jit(solution)/shard_map/psum | solution.py:23
  359.5 176.3 %all-reduce.14.cloned.1.call-start = ((), (), s32[]{:S(2)}) async-start(), calls=%async_computation.15 | async-start | bytes 3538944 | tf_op jit(solution)/shard_map/psum | solution.py:23
  461.1 135.5 %all-reduce.16.cloned.1.call-start = ((), (), s32[]{:S(2)}) async-start(), calls=%async_computation.16 | async-start | bytes 2949120 | tf_op jit(solution)/shard_map/psum | solution.py:278
  469.2 165.4 %reduce-scatter.16.cloned.1.call-start = ((), (), s32[]{:S(2)}) async-start(), calls=%async_computation.21 | async-start | bytes 995328 | tf_op jit(solution)/shard_map/reduce_scatter | solution.py:315
  472.2 200.7 %reduce-scatter.14.cloned.1.call-start = ((), (), s32[]{:S(2)}) async-start(), calls=%async_computation.20 | async-start | bytes 995328 | tf_op jit(solution)/shard_map/reduce_scatter | solution.py:312
  476.0 236.2 %reduce-scatter.12.cloned.1.call-start = ((), (), s32[]{:S(2)}) async-start(), calls=%async_computation.19 | async-start | bytes 995328 | tf_op jit(solution)/shard_map/reduce_scatter | solution.py:309
  547.0 212.3 %reduce-scatter.18.cloned.1.call-start = ((), (), s32[]{:S(2)}) async-start(), calls=%async_computation.22 | async-start | bytes 2985984 | tf_op jit(solution)/shard_map/reduce_scatter | solution.py:318
  551.9 254.9 %reduce-scatter.20.cloned.1.call-start = ((), (), s32[]{:S(2)}) async-start(), calls=%async_computation.23 | async-start | bytes 2985984 | tf_op jit(solution)/shard_map/reduce_scatter | solution.py:321
  556.7 387.1 %all-reduce.18.cloned.1.call-start = ((), (), s32[]{:S(2)}) async-start(), calls=%async_computation.24 | async-start | bytes 7077888 | tf_op jit(solution)/shard_map/psum | solution.py:23
  581.9 417.3 %reduce-scatter.10.cloned.1.call-start = ((), (), s32[]{:S(2)}) async-start(), calls=%async_computation.18 | async-start | bytes 2985984 | tf_op jit(solution)/shard_map/reduce_scatter | solution.py:306
  591.9 466.9 %reduce-scatter.8.cloned.1.call-start = ((), (), s32[]{:S(2)}) async-start(), calls=%async_computation.17 | async-start | bytes 4423680 | tf_op jit(solution)/shard_map/reduce_scatter | solution.py:302
  611.1 332.8 %copy-start.23 = (f32[16,1152]{1,0:T(8,128)S(1)}, f32[16,1152]{1,0:T(8,128)}, u32[]{:S(2)}) copy-start(f32[16,1152]{1,0:T(8,128)} %copy-done.22) | copy-start | bytes 221188
  761.2 184.8 %copy-start.51 = (f32[16,17]{1,0:T(8,128)S(1)}, f32[16,17]{1,0:T(8,128)}, u32[]{:S(2)}) copy-start(f32[16,17]{1,0:T(8,128)} %copy-done.50) | copy-start | bytes 3268
  (60 other events, 465.9 us)
Sparse Core Ops, SparseCore 0:
  10.0 37.6 all-gather.8
  49.5 36.4 all-gather.6
  87.9 26.5 all-gather.10
  122.0 75.7 all-reduce.7
  211.0 74.5 all-reduce.9
  287.3 29.2 all-gather.14
  318.5 30.2 all-gather.12
  359.6 75.5 all-reduce.11
  461.2 74.5 all-reduce.13
  538.9 57.6 all-reduce.15
  600.2 34.3 reduce-scatter.15
  637.7 35.1 reduce-scatter.13
  677.0 35.0 reduce-scatter.11
  715.5 43.7 reduce-scatter.17
  763.0 43.7 reduce-scatter.19
  809.7 134.1 all-reduce.17
  947.2 42.9 reduce-scatter.9
  992.4 66.3 reduce-scatter.7
where the time goes:
time: 1080 us; the launch traced here: 1070 us
  waiting for transfers between devices  733 us (68%)
  matrix products  105 us (10%)
  blocking collectives  95.8 us (9%)
  local copies, waits for them, and re-layouts  71.9 us (7%)
  other arithmetic  45.7 us (4%)
  between operations  15.4 us (1%)
    psum x5, waiting for transfers between devices, total_rows(): return lax.psum(partial_value, 'tp')  407 us
    reduce_scatter x1, waiting for transfers between devices, shards(): lax.psum_scatter(caption_part.astype(jnp.bfloat16), 'tp', scatter_dimensi...  57.7 us
    reduce_scatter x1, waiting for transfers between devices, shards(): lax.psum_scatter(grad_down.astype(jnp.bfloat16), 'seq', scatter_dimension...  45.7 us
    reduce_scatter x1, waiting for transfers between devices, shards(): lax.psum_scatter(grad_up.astype(jnp.bfloat16), 'seq', scatter_dimension=0...  45.6 us
    reduce_scatter x1, waiting for transfers between devices, shards(): lax.psum_scatter(grad_out.astype(jnp.bfloat16), 'seq', scatter_dimension=...  37.7 us
    reduce_scatter x1, waiting for transfers between devices, shards(): lax.psum_scatter(grad_query2.astype(jnp.bfloat16), 'seq', scatter_dimensi...  36.7 us
    all_gather x1, waiting for transfers between devices, shards(): lax.all_gather(w_up, 'seq', axis=0, tiled=True)  28.1 us
    psum x1, blocking collectives, shards(): lax.psum(d_mods.astype(jnp.bfloat16), 'seq').astype(jnp.float32)  24.9 us
  transfers between devices with their start and end apart: 18, of which 15 were waited for; matrix products, arithmetic and copies ran while one was open for 15% of the time, Pallas kernels for 0%

commit v1 on v0

--- a/solution.py
+++ b/solution.py
@@ -20,7 +20,7 @@
 
 
 def total_rows(partial_value):
-    return lax.psum(partial_value, "tp")
+    return jnp.sum(lax.all_gather(partial_value, "tp"), axis=0)
 
 
 def frame_attention(triple, live, head_scale):

time: 1080 us -> 1260 us (1.17)
  waiting for transfers between devices: 733 us -> 902 us
  other arithmetic: 45.7 us -> 71 us
    all_gather x0 -> x6, waiting for transfers between devices: none -> 504 us  [total_rows(): return jnp.sum(lax.all_gather(partial_value, 'tp'), axis=0)]
    psum x5 -> x0, waiting for transfers between devices: 407 us -> none  [total_rows(): return lax.psum(partial_value, 'tp')]
    reduce_scatter x1, waiting for transfers between devices: 0.01 us -> 45.5 us  [shards(): lax.psum_scatter(grad_qkv.astype(jnp.bfloat16), 'seq', scatter_dimension=...]
    reduce_scatter x1, waiting for transfers between devices: 45.6 us -> 13.3 us  [shards(): lax.psum_scatter(grad_up.astype(jnp.bfloat16), 'seq', scatter_dimension=0...]
    psum x1, waiting for transfers between devices: 4.67 us -> 21.5 us  [shards(): lax.psum(kv_grad.astype(jnp.bfloat16), 'seq').astype(jnp.float32)]
    reduce_sum x1 -> x5, other arithmetic: 0.85 us -> 17.6 us  [total_rows(): return jnp.sum(lax.all_gather(partial_value, 'tp'), axis=0)]
    all_gather x1, waiting for transfers between devices: 0.01 us -> 16.8 us  [shards(): lax.all_gather(w_qkv, 'seq', axis=0, tiled=True)]
    all_gather x1, waiting for transfers between devices: 21.8 us -> 35.3 us  [shards(): lax.all_gather(w_ada, 'seq', axis=0, tiled=True)]
  transfers between devices with their start and end apart: 18 -> 19, of which waited for: 15 -> 18; matrix products, arithmetic and copies ran while one was open for 15% -> 13% of each run, Pallas kernels for 0% -> 0%
where the time goes in v1:
time: 1260 us
  waiting for transfers between devices  902 us (72%)
  matrix products  96.7 us (8%)
  blocking collectives  92.3 us (7%)
  local copies, waits for them, and re-layouts  75.5 us (6%)
  other arithmetic  71 us (6%)
  between operations  15.5 us (1%)
    all_gather x6, waiting for transfers between devices, total_rows(): return jnp.sum(lax.all_gather(partial_value, 'tp'), axis=0)  504 us
    reduce_scatter x1, waiting for transfers between devices, shards(): lax.psum_scatter(caption_part.astype(jnp.bfloat16), 'tp', scatter_dimensi...  67.1 us
    reduce_scatter x1, waiting for transfers between devices, shards(): lax.psum_scatter(grad_qkv.astype(jnp.bfloat16), 'seq', scatter_dimension=...  45.5 us
    reduce_scatter x1, waiting for transfers between devices, shards(): lax.psum_scatter(grad_down.astype(jnp.bfloat16), 'seq', scatter_dimension...  45.4 us
    reduce_scatter x1, waiting for transfers between devices, shards(): lax.psum_scatter(grad_query2.astype(jnp.bfloat16), 'seq', scatter_dimensi...  36.6 us
    reduce_scatter x1, waiting for transfers between devices, shards(): lax.psum_scatter(grad_out.astype(jnp.bfloat16), 'seq', scatter_dimension=...  35.5 us
    all_gather x1, waiting for transfers between devices, shards(): lax.all_gather(w_ada, 'seq', axis=0, tiled=True)  35.3 us
    reduce_scatter x1, waiting for transfers between devices, shards(): lax.psum_scatter(grad_out2.astype(jnp.bfloat16), 'seq', scatter_dimension...  33.5 us
  transfers between devices with their start and end apart: 19, of which 18 were waited for; matrix products, arithmetic and copies ran while one was open for 13% of the time, Pallas kernels for 0%

profile of v1, /device:TPU:0, one launch (start us, length us, event | category | flops | bytes accessed | tf_op | source)
XLA Modules:
  0.0 1255.1 jit_solution(18203681360899884402)
XLA Ops:
  13.3 14.3 %all_gather.48 = bf16[288,1152]{0,1:T(8,128)(2,1)S(1)} all-gather(bf16[288,144]{0,1:T(8,128)(2,1)S(1)} %copy-done.49), channel_id=1, replica_groups=mesh['seq'=8,'tp'=4] {'seq'}, dimensions={1}, use_global_device_ids=true | all-gather | bytes 746496 | tf_op jit(solution)/shard_map/all_gather | solution.py:73
  27.6 16.8 %all-gather.19.cloned.1.call-done = bf16[1152,3,288]{2,0,1:T(8,128)(2,1)} async-done(((bf16[144,3,288]{2,0,1:T(8,128)(2,1)}), bf16[1152,3,288]{2,0,1:T(8,128)(2,1)}) %all-gather.19.cloned.1.call-update) | async-done | bytes 1990672 | tf_op jit(solution)/shard_map/all_gather | solution.py:72
  47.4 35.3 %all-gather.17.cloned.1.call-done = bf16[1152,1728]{1,0:T(8,128)(2,1)} async-done(((bf16[144,1728]{1,0:T(8,128)(2,1)}), bf16[1152,1728]{1,0:T(8,128)(2,1)}) %all-gather.17.cloned.1.call-update) | async-done | bytes 3981328 | tf_op jit(solution)/shard_map/all_gather | solution.py:79
  85.6 13.4 %all-gather.4 = f32[4,1728,4]{1,2,0:T(4,128)S(1)} all-gather(f32[1,1728,4]{1,2,0:T(4,128)S(1)} %convolution_bitcast_fusion), channel_id=1, replica_groups=mesh['seq'=8,'tp'=4] {'tp'}, dimensions={0}, use_global_device_ids=true | all-gather | bytes 138240 | tf_op jit(solution)/shard_map/all_gather | solution.py:85
  124.4 10.6 all_gather.51
  135.0 12.4 all_gather.52
  159.8 54.6 %all-gather.31.cloned.1.call-done = f32[64,17,1152]{2,0,1:T(8,128)} async-done(((f32[16,17,1152]{2,0,1:T(8,128)}), f32[64,17,1152]{2,0,1:T(8,128)}) %all-gather.31.cloned.1.call-update) | async-done | bytes 5013520 | tf_op jit(solution)/shard_map/all_gather | solution.py:23
  234.7 91.4 %all-gather.33.cloned.1.call-done = f32[64,17,1152]{2,0,1:T(8,128)} async-done(((f32[16,17,1152]{2,0,1:T(8,128)}), f32[64,17,1152]{2,0,1:T(8,128)}) %all-gather.33.cloned.1.call-update) | async-done | bytes 5013520 | tf_op jit(solution)/shard_map/all_gather | solution.py:23
  340.4 16.2 %all-gather.25.cloned.1.call-done = bf16[1152,1152]{0,1:T(8,128)(2,1)} async-done(((bf16[1152,144]{0,1:T(8,128)(2,1)}), bf16[1152,1152]{0,1:T(8,128)(2,1)}) %all-gather.25.cloned.1.call-update) | async-done | bytes 2654224 | tf_op jit(solution)/shard_map/all_gather | solution.py:78
  360.6 28.1 %all-gather.23.cloned.1.call-done = bf16[1152,1152]{1,0:T(8,128)(2,1)} async-done(((bf16[144,1152]{1,0:T(8,128)(2,1)}), bf16[1152,1152]{1,0:T(8,128)(2,1)}) %all-gather.23.cloned.1.call-update) | async-done | bytes 2654224 | tf_op jit(solution)/shard_map/all_gather | solution.py:77
  403.9 92.7 %all-gather.29.cloned.1.call-done = f32[4,16,17,1152]{3,1,2,0:T(8,128)} async-done(((f32[1,16,17,1152]{3,1,2,0:T(8,128)}), f32[4,16,17,1152]{3,1,2,0:T(8,128)}) %all-gather.29.cloned.1.call-update) | async-done | bytes 5013520 | tf_op jit(solution)/shard_map/all_gather | solution.py:23
  559.7 21.5 %all-reduce.2.cloned.1.call-done = bf16[1200,2,4,72]{0,3,2,1:T(8,128)(2,1)} async-done(((bf16[1200,2,4,72]{0,3,2,1:T(8,128)(2,1)}), bf16[1200,2,4,72]{0,3,2,1:T(8,128)(2,1)}) %all-reduce.2.cloned.1.call-update) | async-done | bytes 1382416 | tf_op jit(solution)/shard_map/psum | solution.py:278
  595.7 80.7 %all-gather.27.cloned.1.call-done = f32[4,16,17,1152]{3,1,2,0:T(8,128)} async-done(((f32[1,16,17,1152]{3,1,2,0:T(8,128)}), f32[4,16,17,1152]{3,1,2,0:T(8,128)}) %all-gather.27.cloned.1.call-update) | async-done | bytes 5013520 | tf_op jit(solution)/shard_map/all_gather | solution.py:23
  680.3 90.4 %all-gather.35.cloned.1.call-done = f32[64,17,1152]{2,0,1:T(8,128)} async-done(((f32[16,17,1152]{2,0,1:T(8,128)}), f32[64,17,1152]{2,0,1:T(8,128)}) %all-gather.35.cloned.1.call-update) | async-done | bytes 5013520 | tf_op jit(solution)/shard_map/all_gather | solution.py:23
  803.4 13.3 %reduce-scatter.18.cloned.1.call-done = bf16[144,1152]{1,0:T(8,128)(2,1)} async-done(((bf16[1152,1152]{1,0:T(8,128)(2,1)}), bf16[144,1152]{1,0:T(8,128)(2,1)}) %reduce-scatter.18.cloned.1.call-update) | async-done | bytes 331792 | tf_op jit(solution)/shard_map/reduce_scatter | solution.py:318
  818.5 45.4 %reduce-scatter.20.cloned.1.call-done = bf16[1152,144]{0,1:T(8,128)(2,1)} async-done(((bf16[1152,1152]{0,1:T(8,128)(2,1)}), bf16[1152,144]{0,1:T(8,128)(2,1)}) %reduce-scatter.20.cloned.1.call-update) | async-done | bytes 331792 | tf_op jit(solution)/shard_map/reduce_scatter | solution.py:321
  868.9 33.5 %reduce-scatter.16.cloned.1.call-done = bf16[288,144]{0,1:T(8,128)(2,1)} async-done(((bf16[288,1152]{0,1:T(8,128)(2,1)}), bf16[288,144]{0,1:T(8,128)(2,1)}) %reduce-scatter.16.cloned.1.call-update) | async-done | bytes 82960 | tf_op jit(solution)/shard_map/reduce_scatter | solution.py:315
  904.1 36.6 %reduce-scatter.14.cloned.1.call-done = bf16[144,288]{1,0:T(8,128)(2,1)} async-done(((bf16[1152,288]{1,0:T(8,128)(2,1)}), bf16[144,288]{1,0:T(8,128)(2,1)}) %reduce-scatter.14.cloned.1.call-update) | async-done | bytes 82960 | tf_op jit(solution)/shard_map/reduce_scatter | solution.py:312
  942.3 67.1 %reduce-scatter.8.cloned.1.call-done = bf16[4,300,288]{1,2,0:T(8,128)(2,1)} async-done(((bf16[4,300,1152]{1,2,0:T(8,128)(2,1)}), bf16[4,300,288]{1,2,0:T(8,128)(2,1)}) %reduce-scatter.8.cloned.1.call-update) | async-done | bytes 691216 | tf_op jit(solution)/shard_map/reduce_scatter | solution.py:302
  1012.7 35.5 %reduce-scatter.12.cloned.1.call-done = bf16[288,144]{0,1:T(8,128)(2,1)} async-done(((bf16[288,1152]{0,1:T(8,128)(2,1)}), bf16[288,144]{0,1:T(8,128)(2,1)}) %reduce-scatter.12.cloned.1.call-update) | async-done | bytes 82960 | tf_op jit(solution)/shard_map/reduce_scatter | solution.py:309
  1049.8 45.5 %reduce-scatter.10.cloned.1.call-done = bf16[144,3,288]{2,0,1:T(8,128)(2,1)} async-done(((bf16[1152,3,288]{2,0,1:T(8,128)(2,1)}), bf16[144,3,288]{2,0,1:T(8,128)(2,1)}) %reduce-scatter.10.cloned.1.call-update) | async-done | bytes 248848 | tf_op jit(solution)/shard_map/reduce_scatter | solution.py:306
  1097.2 94.1 %all-gather.37.cloned.1.call-done = f32[64,17,1152]{2,0,1:T(8,128)} async-done(((f32[16,17,1152]{2,0,1:T(8,128)}), f32[64,17,1152]{2,0,1:T(8,128)}) %all-gather.37.cloned.1.call-update) | async-done | bytes 5013520 | tf_op jit(solution)/shard_map/all_gather | solution.py:23
  1201.1 24.6 %psum.22 = bf16[4,6912]{1,0:T(4,128)(2,1)S(1)} all-reduce(bf16[4,6912]{1,0:T(4,128)(2,1)S(1)} %bitcast.210), channel_id=1, replica_groups=mesh['seq'=8,'tp'=4] {'seq'}, use_global_device_ids=true, to_apply=%region_31.32 | all-reduce | flops 27648 | bytes 110592 | tf_op jit(solution)/shard_map/psum | solution.py:279
  1231.1 17.0 %psum.23 = f32[4,1152]{1,0:T(4,128)} all-reduce(f32[4,1152]{1,0:T(4,128)S(1)} %fusion.78), channel_id=1, replica_groups=mesh['seq'=8,'tp'=4] {'tp'}, use_global_device_ids=true, to_apply=%region_32.33 | all-reduce | flops 4608 | bytes 36864 | tf_op jit(solution)/shard_map/psum | solution.py:291
  (319 shorter events, 248.6 us)
Async XLA Ops:
  7.2 37.2 %all-gather.19.cloned.1.call-start = ((), (), s32[]{:S(2)}) async-start(), calls=%async_computation.8 | async-start | bytes 2985984 | tf_op jit(solution)/shard_map/all_gather | solution.py:72
  7.9 74.8 %all-gather.17.cloned.1.call-start = ((), (), s32[]{:S(2)}) async-start(), calls=%async_computation.7 | async-start | bytes 4644864 | tf_op jit(solution)/shard_map/all_gather | solution.py:79
  8.7 139.1 %all-gather.21.cloned.1.call-start = ((), (), s32[]{:S(2)}) async-start(), calls=%async_computation.9 | async-start | bytes 1990656 | tf_op jit(solution)/shard_map/all_gather | solution.py:75
  9.4 205.0 %all-gather.31.cloned.1.call-start = ((), (), s32[]{:S(2)}) async-start(), calls=%async_computation.22 | async-start | bytes 6266880 | tf_op jit(solution)/shard_map/all_gather | solution.py:23
  12.6 34.8 %copy-start.53 = (f32[16,17]{1,0:T(8,128)}, f32[16,17]{1,0:T(8,128)S(1)}, u32[]{:S(2)}) copy-start(f32[16,17]{1,0:T(8,128)S(1)} %fusion.34) | copy-start | bytes 3268
  27.6 90.8 %copy-start.9 = (bf16[288,1152]{0,1:T(8,128)(2,1)}, bf16[288,1152]{0,1:T(8,128)(2,1)S(1)}, u32[]{:S(2)}) copy-start(bf16[288,1152]{0,1:T(8,128)(2,1)S(1)} %all_gather.48) | copy-start | bytes 1990660
  47.4 61.6 %copy-start.7 = (bf16[1152,3,288]{0,2,1:T(8,128)(2,1)}, bf16[1152,3,288]{0,2,1:T(8,128)(2,1)S(1)}, u32[]{:S(2)}) copy-start(bf16[1152,3,288]{0,2,1:T(8,128)(2,1)S(1)} %copy.168) | copy-start | bytes 5971972
  120.1 206.1 %all-gather.33.cloned.1.call-start = ((), (), s32[]{:S(2)}) async-start(), calls=%async_computation.23 | async-start | bytes 6266880 | tf_op jit(solution)/shard_map/all_gather | solution.py:23
  233.3 123.2 %all-gather.25.cloned.1.call-start = ((), (), s32[]{:S(2)}) async-start(), calls=%async_computation.11 | async-start | bytes 2985984 | tf_op jit(solution)/shard_map/all_gather | solution.py:78
  233.9 154.8 %all-gather.23.cloned.1.call-start = ((), (), s32[]{:S(2)}) async-start(), calls=%async_computation.10 | async-start | bytes 2985984 | tf_op jit(solution)/shard_map/all_gather | solution.py:77
  234.7 261.9 %all-gather.29.cloned.1.call-start = ((), (), s32[]{:S(2)}) async-start(), calls=%async_computation.13 | async-start | bytes 6266880 | tf_op jit(solution)/shard_map/all_gather | solution.py:23
  402.2 179.1 %all-reduce.2.cloned.1.call-start = ((), (), s32[]{:S(2)}) async-start(), calls=%async_computation.14 | async-start | bytes 2949120 | tf_op jit(solution)/shard_map/psum | solution.py:278
  524.2 152.2 %all-gather.27.cloned.1.call-start = ((), (), s32[]{:S(2)}) async-start(), calls=%async_computation.12 | async-start | bytes 6266880 | tf_op jit(solution)/shard_map/all_gather | solution.py:23
  534.1 236.6 %all-gather.35.cloned.1.call-start = ((), (), s32[]{:S(2)}) async-start(), calls=%async_computation.24 | async-start | bytes 6266880 | tf_op jit(solution)/shard_map/all_gather | solution.py:23
  544.4 272.3 %reduce-scatter.18.cloned.1.call-start = ((), (), s32[]{:S(2)}) async-start(), calls=%async_computation.20 | async-start | bytes 2985984 | tf_op jit(solution)/shard_map/reduce_scatter | solution.py:318
  549.2 314.8 %reduce-scatter.20.cloned.1.call-start = ((), (), s32[]{:S(2)}) async-start(), calls=%async_computation.21 | async-start | bytes 2985984 | tf_op jit(solution)/shard_map/reduce_scatter | solution.py:321
  554.8 347.6 %reduce-scatter.16.cloned.1.call-start = ((), (), s32[]{:S(2)}) async-start(), calls=%async_computation.19 | async-start | bytes 995328 | tf_op jit(solution)/shard_map/reduce_scatter | solution.py:315
  557.9 382.8 %reduce-scatter.14.cloned.1.call-start = ((), (), s32[]{:S(2)}) async-start(), calls=%async_computation.18 | async-start | bytes 995328 | tf_op jit(solution)/shard_map/reduce_scatter | solution.py:312
  559.7 449.7 %reduce-scatter.8.cloned.1.call-start = ((), (), s32[]{:S(2)}) async-start(), calls=%async_computation.15 | async-start | bytes 4423680 | tf_op jit(solution)/shard_map/reduce_scatter | solution.py:302
  592.1 456.1 %reduce-scatter.12.cloned.1.call-start = ((), (), s32[]{:S(2)}) async-start(), calls=%async_computation.17 | async-start | bytes 995328 | tf_op jit(solution)/shard_map/reduce_scatter | solution.py:309
  789.3 306.1 %reduce-scatter.10.cloned.1.call-start = ((), (), s32[]{:S(2)}) async-start(), calls=%async_computation.16 | async-start | bytes 2985984 | tf_op jit(solution)/shard_map/reduce_scatter | solution.py:306
  797.9 393.4 %all-gather.37.cloned.1.call-start = ((), (), s32[]{:S(2)}) async-start(), calls=%async_computation.25 | async-start | bytes 6266880 | tf_op jit(solution)/shard_map/all_gather | solution.py:23
  803.3 62.4 %copy-start.13 = (bf16[1200,2,4,72]{0,3,2,1:T(8,128)(2,1)S(1)}, bf16[1200,2,4,72]{0,3,2,1:T(8,128)(2,1)}, u32[]{:S(2)}) copy-start(bf16[1200,2,4,72]{0,3,2,1:T(8,128)(2,1)} %all-reduce.2.cloned.1.call-done) | copy-start | bytes 4147204
  868.9 142.9 %copy-start.18 = (bf16[16,17,1152]{2,1,0:T(8,128)(2,1)S(1)}, bf16[16,17,1152]{2,1,0:T(8,128)(2,1)}, u32[]{:S(2)}) copy-start(bf16[16,17,1152]{2,1,0:T(8,128)(2,1)} %get-tuple-element.145) | copy-start | bytes 1880068
  (63 other events, 176.1 us)
Sparse Core Ops, SparseCore 0:
  9.9 34.3 all-gather.18
  46.3 36.4 all-gather.16
  84.6 26.5 all-gather.20
  120.2 94.2 all-gather.30
  233.5 92.6 all-gather.32
  327.9 28.6 all-gather.24
  358.4 30.2 all-gather.22
  402.3 94.2 all-gather.28
  524.3 56.9 all-reduce.1
  582.8 93.5 all-gather.26
  678.0 92.6 all-gather.34
  774.5 42.1 reduce-scatter.17
  820.1 43.7 reduce-scatter.19
  867.3 35.0 reduce-scatter.15
  905.5 35.0 reduce-scatter.13
  943.0 66.3 reduce-scatter.7
  1012.8 35.4 reduce-scatter.11
  1051.6 43.7 reduce-scatter.9
  1097.0 94.2 all-gather.36
